TPU v7x, 32 devices: a whole 2x2x4 slice. The times are simulated.
32 devices in a mesh: gx: 8 (over y, x, core), gz: 4 (over z).
Axes of the slice: x: 2, y: 2, z: 4, core: 2. Of those that a mesh axis runs over, the one named last changes fastest.
Arguments:
- velocity_old: float32 [3, 64, 64, 128], P(None, 'gx', 'gz'), may hold values from -6 to 6
- source: float32 [3, 64, 64, 128], P(None, 'gx', 'gz'), may hold values from -6 to 6
- diag_coef: float32 [64, 64, 128], P('gx', 'gz'), may hold values from 0.5 to 2
- face_coef: float32 [3, 64, 64, 128], P(None, 'gx', 'gz'), may hold values from 0.2 to 2
- bc_flags: int32 [2, 64, 64], P(None, 'gx', 'gz'), may hold values from 0 to 1
- coarse_map: int32 [64, 64, 128], P('gx', 'gz'), may hold values from 0 to 15
- coarse_inverse: float32 [512, 64], P('gx'), may hold values from -0.1 to 0.3
Outputs:
- velocity: float32 [3, 64, 64, 128], P(None, 'gx', 'gz')
- pressure: float32 [64, 64, 128], P('gx', 'gz')
All inputs are finite; a program needn't handle non-finite values.
Results may differ from a plain program's by a relative error of at most 0.0003.
Values sent between devices are 32-bit elements; how exact they have to be, the bound alone decides.
A program may use at most 64 MiB of HBM per device.

v0:
```python
import jax
import jax.numpy as jnp
from jax import lax
from jax.sharding import PartitionSpec as P

COARSE = 16
jacobi_weight = 2.0 / 3.0


def passed_along(value, axis, steps):
    count = lax.axis_size(axis)
    pairs = [(source, (source + steps) % count) for source in range(count)]
    return lax.ppermute(value, axis, pairs)


def with_halo(array, sides, width):
    for axis, dim in sides:
        count, length = (lax.axis_size(axis), array.shape[dim])
        up = [(i, (i + 1) % count) for i in range(count)]
        down = [(j, i) for i, j in up]
        last = lax.slice_in_dim(array, length - width, length, axis=dim)
        initial = lax.slice_in_dim(array, 0, width, axis=dim)
        before = lax.ppermute(last, axis, up)
        after = lax.ppermute(initial, axis, down)
        array = jnp.concatenate([before, array, after], axis=dim)
    return array


def inner_local(left, right):
    return jnp.sum(left * right, axis=(1, 2, 3))


def widen(value):
    return value[:, None, None, None]


def global_sums(pairs):
    local = jnp.stack([inner_local(left, right) for left, right in pairs])
    return lax.psum(local, ("gx", "gz"))


def solve_values(velocity_old, source, diag_coef, face_coef):
    coef_x, coef_z, coef_y = (face_coef[0], face_coef[1], face_coef[2])
    count_y = coef_y.shape[-1]
    level = lax.broadcasted_iota(jnp.int32, coef_y.shape, 2)
    wall = jnp.where((level == 0) | (level == count_y - 1), coef_y[..., -1:], 0.0)
    west_cx = passed_along(coef_x[-1:], "gx", 1)
    south_cz = passed_along(coef_z[:, -1:], "gz", 1)
    wide_cx = jnp.concatenate([west_cx, coef_x], 0)
    wide_cz = jnp.concatenate([south_cz, coef_z], 1)

    def apply(field):
        padded = with_halo(field, (("gx", 1), ("gz", 2)), 1)
        flux_x = wide_cx * (padded[:, :-1, 1:-1] - padded[:, 1:, 1:-1])
        flux_z = wide_cz * (padded[:, 1:-1, :-1] - padded[:, 1:-1, 1:])
        planar = flux_x[:, 1:] - flux_x[:, :-1] + (flux_z[:, :, 1:] - flux_z[:, :, :-1])
        grad_y = coef_y[..., :-1] * (field[..., :-1] - field[..., 1:])
        zero = jnp.zeros_like(field[..., :1])
        vertical = (
            jnp.concatenate([grad_y, zero], -1) - jnp.concatenate([zero, grad_y], -1) + wall * field
        )
        return diag_coef * field + planar + vertical

    x = velocity_old
    r = source - apply(x)
    r0 = r
    p = r
    v = apply(p)
    first = global_sums([(r0, r0), (r0, v)])
    rho = first[0]
    alpha = rho / first[1]
    s = r - widen(alpha) * v
    t = apply(s)
    second = global_sums([(t, s), (t, t), (r0, s), (r0, t)])
    omega = second[0] / second[1]
    x = x + widen(alpha) * p + widen(omega) * s
    r = s - widen(omega) * t
    rho_new = second[2] - omega * second[3]
    beta = rho_new / rho * (alpha / omega)
    p = r + widen(beta) * (p - widen(omega) * v)
    v = apply(p)
    third = global_sums([(r0, v)])
    alpha = rho_new / third[0]
    s = r - widen(alpha) * v
    t = apply(s)
    fourth = global_sums([(t, s), (t, t)])
    omega = fourth[0] / fourth[1]
    return x + widen(alpha) * p + widen(omega) * s


def body(velocity_old, source, diag_coef, face_coef, bc_flags, coarse_map, coarse_inverse):
    coef_y = face_coef[2]
    count_y = coef_y.shape[-1]
    level = lax.broadcasted_iota(jnp.int32, coef_y.shape, 2)
    velocity = solve_values(velocity_old, source, diag_coef, face_coef)
    along_x, along_z, along_y = (velocity[0], velocity[1], velocity[2])
    west_u = passed_along(along_x[-1:], "gx", 1)
    south_w = passed_along(along_z[:, -1:], "gz", 1)
    zero = jnp.zeros_like(along_y[..., :1])
    div = (
        along_x
        - jnp.concatenate([west_u, along_x[:-1]], 0)
        + (along_z - jnp.concatenate([south_w, along_z[:, :-1]], 1))
    )
    div = div + (along_y - jnp.concatenate([zero, along_y[..., :-1]], -1))
    flags = bc_flags.astype(jnp.float32)
    bottom = level == 0
    top = level == count_y - 1
    pdiag = 6.0 - bottom.astype(jnp.float32) - top.astype(jnp.float32)
    pdiag = (
        pdiag
        + jnp.where(bottom, flags[0][..., None], 0.0)
        + jnp.where(top, flags[1][..., None], 0.0)
    )

    def pressure_apply(field):
        padded = with_halo(field, (("gx", 0), ("gz", 1)), 1)
        beside = padded[2:, 1:-1] + padded[:-2, 1:-1] + (padded[1:-1, 2:] + padded[1:-1, :-2])
        beside = beside + (
            jnp.concatenate([field[..., 1:], zero], -1)
            + jnp.concatenate([zero, field[..., :-1]], -1)
        )
        return pdiag * field - beside

    q = jacobi_weight * div / pdiag
    q = q + jacobi_weight * (div - pressure_apply(q)) / pdiag
    res = div - pressure_apply(q)
    labels = lax.broadcasted_iota(jnp.int32, (COARSE, 1, 1, 1), 0)
    onehot = (coarse_map[None] == labels).astype(jnp.float32)
    coarse = jnp.einsum("kxzy,xzy->k", onehot, res, precision=lax.Precision.HIGHEST)
    offset = lax.axis_index("gz") * COARSE
    columns = lax.dynamic_slice_in_dim(coarse_inverse, offset, COARSE, 1)
    own = lax.psum_scatter(
        jnp.dot(columns, coarse, precision=lax.Precision.HIGHEST),
        "gz",
        scatter_dimension=0,
        tiled=True,
    )
    q = q + jnp.einsum("kxzy,k->xzy", onehot, own, precision=lax.Precision.HIGHEST)
    for sweep in range(2):
        q = q + jacobi_weight * (div - pressure_apply(q)) / pdiag
    return (velocity, q)


def solution(mesh):
    placed = (
        P(None, "gx", "gz", None),
        P(None, "gx", "gz", None),
        P("gx", "gz", None),
        P(None, "gx", "gz", None),
        P(None, "gx", "gz"),
        P("gx", "gz", None),
        P("gx", None),
    )
    return jax.shard_map(
        body,
        mesh=mesh,
        in_specs=placed,
        out_specs=(P(None, "gx", "gz", None), P("gx", "gz", None)),
        check_vma=False,
    )
```

profile of v0, /device:TPU:0, one launch (start us, length us, event | category | flops | bytes accessed | tf_op | source)
XLA Modules:
  0.0 278.5 jit_solution(2390331848632894776)
XLA Ops:
  1.6 3.1 %collective-permute-start.3 = (f32[8,1,128]{2,1,0:T(1,128)S(1)}, f32[8,1,128]{2,1,0:T(1,128)S(1)}, u32[]{:S(2)}, u32[]{:S(2)}) collective-permute-start(f32[8,1,128]{2,1,0:T(1,128)S(1)} %slice.567), channel_id=1, source_target_pairs={{0,1},{1,2},{2,3},{3,0},{4,5},{5,6},{6,7},{7,4},{8,9},{9,10},{10,1... | collective-permute-start | bytes 12296 | tf_op jit(solution)/shard_map/ppermute | solution.py:13
  4.8 2.6 collective-permute-start.2
  9.5 2.6 collective-permute-done
  13.8 2.2 collective-permute-start.5
  18.1 2.6 collective-permute-start.7
  23.9 2.5 collective-permute-start.9
  28.4 39.4 %psum.28 = f32[2,3]{1,0:T(2,128)S(1)} all-reduce(f32[2,3]{1,0:T(2,128)S(1)} %pad_maximum_fusion.85), channel_id=1, replica_groups=mesh['gx'=8,'gz'=4] {'gx','gz'}, use_global_device_ids=true, to_apply=%region_2.3 | all-reduce | flops 6 | bytes 48 | tf_op jit(solution)/shard_map/psum | solution.py:39
  68.0 2.6 collective-permute-start.11
  78.3 39.7 %psum.29 = f32[4,3]{1,0:T(4,128)S(1)} all-reduce(f32[4,3]{1,0:T(4,128)S(1)} %pad_maximum_fusion.84), channel_id=1, replica_groups=mesh['gx'=8,'gz'=4] {'gx','gz'}, use_global_device_ids=true, to_apply=%region_7.8 | all-reduce | flops 12 | bytes 96 | tf_op jit(solution)/shard_map/psum | solution.py:39
  118.2 2.6 collective-permute-start.15
  122.4 2.1 collective-permute-start.16
  128.5 40.0 %psum.30 = f32[3]{0:T(128)S(1)} all-reduce(f32[3]{0:T(128)S(1)} %get-tuple-element.12), channel_id=1, replica_groups=mesh['gx'=8,'gz'=4] {'gx','gz'}, use_global_device_ids=true, to_apply=%region_9.10 | all-reduce | flops 3 | bytes 24 | tf_op jit(solution)/shard_map/psum | solution.py:39
  168.7 2.6 collective-permute-start.19
  179.0 39.7 %psum.31 = f32[2,3]{1,0:T(2,128)S(1)} all-reduce(f32[2,3]{1,0:T(2,128)S(1)} %pad_maximum_fusion.86), channel_id=1, replica_groups=mesh['gx'=8,'gz'=4] {'gx','gz'}, use_global_device_ids=true, to_apply=%region_12.13 | all-reduce | flops 6 | bytes 48 | tf_op jit(solution)/shard_map/psum | solution.py:39
  218.9 2.1 collective-permute-start.23
  221.0 3.3 %collective-permute-done.23 = f32[8,1,128]{2,1,0:T(1,128)S(1)} collective-permute-done((f32[8,1,128]{2,1,0:T(1,128)S(1)}, f32[8,1,128]{2,1,0:T(1,128)S(1)}, u32[]{:S(2)}, u32[]{:S(2)}) %collective-permute-start.23) | collective-permute-done | bytes 4128 | tf_op jit(solution)/shard_map/ppermute | solution.py:13
  226.6 2.6 collective-permute-done.25
  232.9 3.5 %collective-permute-done.27 = f32[10,1,128]{2,1,0:T(1,128)S(1)} collective-permute-done((f32[10,1,128]{2,1,0:T(1,128)S(1)}, f32[10,1,128]{2,1,0:T(1,128)S(1)}, u32[]{:S(2)}, u32[]{:S(2)}) %collective-permute-start.27) | collective-permute-done | bytes 5152 | tf_op jit(solution)/shard_map/ppermute | solution.py:23
  240.8 2.0 collective-permute-start.31
  247.4 8.5 %all-reduce.19 = f32[64]{0:T(128)S(1)} all-reduce(f32[64]{0:T(128)S(1)} %convolution_bitcast_fusion), channel_id=2, replica_groups=mesh['gx'=8,'gz'=4] {'gz'}, use_global_device_ids=true, to_apply=%region_13.14.clone | all-reduce | flops 64 | bytes 512
  257.9 2.7 collective-permute-done.33
  264.3 3.7 %collective-permute-done.35 = f32[10,1,128]{2,1,0:T(1,128)S(1)} collective-permute-done((f32[10,1,128]{2,1,0:T(1,128)S(1)}, f32[10,1,128]{2,1,0:T(1,128)S(1)}, u32[]{:S(2)}, u32[]{:S(2)}) %collective-permute-start.35) | collective-permute-done | bytes 5152 | tf_op jit(solution)/shard_map/ppermute | solution.py:23
  269.5 2.7 collective-permute-done.37
  272.2 2.0 collective-permute-start.39
  (163 shorter events, 58.9 us)
Async XLA Ops:
  1.6 7.8 %collective-permute-start.3 = (f32[8,1,128]{2,1,0:T(1,128)S(1)}, f32[8,1,128]{2,1,0:T(1,128)S(1)}, u32[]{:S(2)}, u32[]{:S(2)}) collective-permute-start(f32[8,1,128]{2,1,0:T(1,128)S(1)} %slice.567), channel_id=1, source_target_pairs={{0,1},{1,2},{2,3},{3,0},{4,5},{5,6},{6,7},{7,4},{8,9},{9,10},{10,1... | collective-permute-start | bytes 12296 | tf_op jit(solution)/shard_map/ppermute | solution.py:13
  4.7 7.3 %collective-permute-start.1 = (f32[3,1,16,128]{3,2,1,0:T(8,128)S(1)}, f32[3,1,16,128]{3,2,1,0:T(8,128)S(1)}, u32[]{:S(2)}, u32[]{:S(2)}) collective-permute-start(f32[3,1,16,128]{3,2,1,0:T(8,128)S(1)} %get-tuple-element.42), channel_id=1, source_target_pairs={{0,4},{4,8},{8,12},{12,16},{16,20},{20,24},{24,28},{28,0},{1,5},{5... | collective-permute-start | bytes 73736 | tf_op jit(solution)/shard_map/ppermute | solution.py:23
  4.8 7.4 %collective-permute-start.2 = (f32[3,1,16,128]{3,2,1,0:T(8,128)S(1)}, f32[3,1,16,128]{3,2,1,0:T(8,128)S(1)}, u32[]{:S(2)}, u32[]{:S(2)}) collective-permute-start(f32[3,1,16,128]{3,2,1,0:T(8,128)S(1)} %get-tuple-element.41), channel_id=1, source_target_pairs={{4,0},{8,4},{12,8},{16,12},{20,16},{24,20},{28,24},{0,28},{5,1},{9... | collective-permute-start | bytes 73736 | tf_op jit(solution)/shard_map/ppermute | solution.py:24
  12.2 5.6 %collective-permute-start.4 = (f32[3,10,1,128]{3,2,1,0:T(1,128)S(1)}, f32[3,10,1,128]{3,2,1,0:T(1,128)S(1)}, u32[]{:S(2)}, u32[]{:S(2)}) collective-permute-start(f32[3,10,1,128]{3,2,1,0:T(1,128)S(1)} %get-tuple-element.26), channel_id=1, source_target_pairs={{0,1},{1,2},{2,3},{3,0},{4,5},{5,6},{6,7},{7,4},{8,9},{9,10},{10,1... | collective-permute-start | bytes 46088 | tf_op jit(solution)/shard_map/ppermute | solution.py:23
  18.0 4.4 %collective-permute-start.6 = (f32[3,1,16,128]{3,2,1,0:T(8,128)S(1)}, f32[3,1,16,128]{3,2,1,0:T(8,128)S(1)}, u32[]{:S(2)}, u32[]{:S(2)}) collective-permute-start(f32[3,1,16,128]{3,2,1,0:T(8,128)S(1)} %get-tuple-element.36), channel_id=1, source_target_pairs={{0,4},{4,8},{8,12},{12,16},{16,20},{20,24},{24,28},{28,0},{1,5},{5... | collective-permute-start | bytes 73736 | tf_op jit(solution)/shard_map/ppermute | solution.py:23
  18.1 4.4 %collective-permute-start.7 = (f32[3,1,16,128]{3,2,1,0:T(8,128)S(1)}, f32[3,1,16,128]{3,2,1,0:T(8,128)S(1)}, u32[]{:S(2)}, u32[]{:S(2)}) collective-permute-start(f32[3,1,16,128]{3,2,1,0:T(8,128)S(1)} %get-tuple-element.37), channel_id=1, source_target_pairs={{4,0},{8,4},{12,8},{16,12},{20,16},{24,20},{28,24},{0,28},{5,1},{9... | collective-permute-start | bytes 73736 | tf_op jit(solution)/shard_map/ppermute | solution.py:24
  22.5 5.6 %collective-permute-start.8 = (f32[3,10,1,128]{3,2,1,0:T(1,128)S(1)}, f32[3,10,1,128]{3,2,1,0:T(1,128)S(1)}, u32[]{:S(2)}, u32[]{:S(2)}) collective-permute-start(f32[3,10,1,128]{3,2,1,0:T(1,128)S(1)} %get-tuple-element.24), channel_id=1, source_target_pairs={{0,1},{1,2},{2,3},{3,0},{4,5},{5,6},{6,7},{7,4},{8,9},{9,10},{10,1... | collective-permute-start | bytes 46088 | tf_op jit(solution)/shard_map/ppermute | solution.py:23
  23.9 4.2 %collective-permute-start.9 = (f32[3,10,1,128]{3,2,1,0:T(1,128)S(1)}, f32[3,10,1,128]{3,2,1,0:T(1,128)S(1)}, u32[]{:S(2)}, u32[]{:S(2)}) collective-permute-start(f32[3,10,1,128]{3,2,1,0:T(1,128)S(1)} %get-tuple-element.25), channel_id=1, source_target_pairs={{1,0},{2,1},{3,2},{0,3},{5,4},{6,5},{7,6},{4,7},{9,8},{10,9},{11,1... | collective-permute-start | bytes 46088 | tf_op jit(solution)/shard_map/ppermute | solution.py:24
  67.9 4.2 %collective-permute-start.10 = (f32[3,1,16,128]{3,2,1,0:T(8,128)S(1)}, f32[3,1,16,128]{3,2,1,0:T(8,128)S(1)}, u32[]{:S(2)}, u32[]{:S(2)}) collective-permute-start(f32[3,1,16,128]{3,2,1,0:T(8,128)S(1)} %get-tuple-element.34), channel_id=1, source_target_pairs={{0,4},{4,8},{8,12},{12,16},{16,20},{20,24},{24,28},{28,0},{1,5},{5... | collective-permute-start | bytes 73736 | tf_op jit(solution)/shard_map/ppermute | solution.py:23
  68.0 4.2 %collective-permute-start.11 = (f32[3,1,16,128]{3,2,1,0:T(8,128)S(1)}, f32[3,1,16,128]{3,2,1,0:T(8,128)S(1)}, u32[]{:S(2)}, u32[]{:S(2)}) collective-permute-start(f32[3,1,16,128]{3,2,1,0:T(8,128)S(1)} %get-tuple-element.35), channel_id=1, source_target_pairs={{4,0},{8,4},{12,8},{16,12},{20,16},{24,20},{28,24},{0,28},{5,1},{9... | collective-permute-start | bytes 73736 | tf_op jit(solution)/shard_map/ppermute | solution.py:24
  72.2 5.6 %collective-permute-start.12 = (f32[3,10,1,128]{3,2,1,0:T(1,128)S(1)}, f32[3,10,1,128]{3,2,1,0:T(1,128)S(1)}, u32[]{:S(2)}, u32[]{:S(2)}) collective-permute-start(f32[3,10,1,128]{3,2,1,0:T(1,128)S(1)} %get-tuple-element.22), channel_id=1, source_target_pairs={{0,1},{1,2},{2,3},{3,0},{4,5},{5,6},{6,7},{7,4},{8,9},{9,10},{10,1... | collective-permute-start | bytes 46088 | tf_op jit(solution)/shard_map/ppermute | solution.py:23
  118.1 4.2 %collective-permute-start.14 = (f32[3,1,16,128]{3,2,1,0:T(8,128)S(1)}, f32[3,1,16,128]{3,2,1,0:T(8,128)S(1)}, u32[]{:S(2)}, u32[]{:S(2)}) collective-permute-start(f32[3,1,16,128]{3,2,1,0:T(8,128)S(1)} %get-tuple-element.32), channel_id=1, source_target_pairs={{0,4},{4,8},{8,12},{12,16},{16,20},{20,24},{24,28},{28,0},{1,5},{5... | collective-permute-start | bytes 73736 | tf_op jit(solution)/shard_map/ppermute | solution.py:23
  118.2 4.2 %collective-permute-start.15 = (f32[3,1,16,128]{3,2,1,0:T(8,128)S(1)}, f32[3,1,16,128]{3,2,1,0:T(8,128)S(1)}, u32[]{:S(2)}, u32[]{:S(2)}) collective-permute-start(f32[3,1,16,128]{3,2,1,0:T(8,128)S(1)} %get-tuple-element.33), channel_id=1, source_target_pairs={{4,0},{8,4},{12,8},{16,12},{20,16},{24,20},{28,24},{0,28},{5,1},{9... | collective-permute-start | bytes 73736 | tf_op jit(solution)/shard_map/ppermute | solution.py:24
  122.4 5.6 %collective-permute-start.16 = (f32[3,10,1,128]{3,2,1,0:T(1,128)S(1)}, f32[3,10,1,128]{3,2,1,0:T(1,128)S(1)}, u32[]{:S(2)}, u32[]{:S(2)}) collective-permute-start(f32[3,10,1,128]{3,2,1,0:T(1,128)S(1)} %get-tuple-element.20), channel_id=1, source_target_pairs={{0,1},{1,2},{2,3},{3,0},{4,5},{5,6},{6,7},{7,4},{8,9},{9,10},{10,1... | collective-permute-start | bytes 46088 | tf_op jit(solution)/shard_map/ppermute | solution.py:23
  168.6 4.2 %collective-permute-start.18 = (f32[3,1,16,128]{3,2,1,0:T(8,128)S(1)}, f32[3,1,16,128]{3,2,1,0:T(8,128)S(1)}, u32[]{:S(2)}, u32[]{:S(2)}) collective-permute-start(f32[3,1,16,128]{3,2,1,0:T(8,128)S(1)} %get-tuple-element.30), channel_id=1, source_target_pairs={{0,4},{4,8},{8,12},{12,16},{16,20},{20,24},{24,28},{28,0},{1,5},{5... | collective-permute-start | bytes 73736 | tf_op jit(solution)/shard_map/ppermute | solution.py:23
  168.7 4.2 %collective-permute-start.19 = (f32[3,1,16,128]{3,2,1,0:T(8,128)S(1)}, f32[3,1,16,128]{3,2,1,0:T(8,128)S(1)}, u32[]{:S(2)}, u32[]{:S(2)}) collective-permute-start(f32[3,1,16,128]{3,2,1,0:T(8,128)S(1)} %get-tuple-element.31), channel_id=1, source_target_pairs={{4,0},{8,4},{12,8},{16,12},{20,16},{24,20},{28,24},{0,28},{5,1},{9... | collective-permute-start | bytes 73736 | tf_op jit(solution)/shard_map/ppermute | solution.py:24
  172.9 5.6 %collective-permute-start.20 = (f32[3,10,1,128]{3,2,1,0:T(1,128)S(1)}, f32[3,10,1,128]{3,2,1,0:T(1,128)S(1)}, u32[]{:S(2)}, u32[]{:S(2)}) collective-permute-start(f32[3,10,1,128]{3,2,1,0:T(1,128)S(1)} %get-tuple-element.18), channel_id=1, source_target_pairs={{0,1},{1,2},{2,3},{3,0},{4,5},{5,6},{6,7},{7,4},{8,9},{9,10},{10,1... | collective-permute-start | bytes 46088 | tf_op jit(solution)/shard_map/ppermute | solution.py:23
  218.9 5.5 %collective-permute-start.23 = (f32[8,1,128]{2,1,0:T(1,128)S(1)}, f32[8,1,128]{2,1,0:T(1,128)S(1)}, u32[]{:S(2)}, u32[]{:S(2)}) collective-permute-start(f32[8,1,128]{2,1,0:T(1,128)S(1)} %slice.610), channel_id=1, source_target_pairs={{0,1},{1,2},{2,3},{3,0},{4,5},{5,6},{6,7},{7,4},{8,9},{9,10},{10,1... | collective-permute-start | bytes 12296 | tf_op jit(solution)/shard_map/ppermute | solution.py:13
  231.1 5.4 %collective-permute-start.27 = (f32[10,1,128]{2,1,0:T(1,128)S(1)}, f32[10,1,128]{2,1,0:T(1,128)S(1)}, u32[]{:S(2)}, u32[]{:S(2)}) collective-permute-start(f32[10,1,128]{2,1,0:T(1,128)S(1)} %get-tuple-element.50), channel_id=1, source_target_pairs={{0,1},{1,2},{2,3},{3,0},{4,5},{5,6},{6,7},{7,4},{8,9},{9,10},{10,1... | collective-permute-start | bytes 15368 | tf_op jit(solution)/shard_map/ppermute | solution.py:23
  236.7 4.0 %collective-permute-start.29 = (f32[1,16,128]{2,1,0:T(8,128)S(1)}, f32[1,16,128]{2,1,0:T(8,128)S(1)}, u32[]{:S(2)}, u32[]{:S(2)}) collective-permute-start(f32[1,16,128]{2,1,0:T(8,128)S(1)} %get-tuple-element.61), channel_id=1, source_target_pairs={{0,4},{4,8},{8,12},{12,16},{16,20},{20,24},{24,28},{28,0},{1,5},{5... | collective-permute-start | bytes 24584 | tf_op jit(solution)/shard_map/ppermute | solution.py:23
  240.8 5.5 %collective-permute-start.31 = (f32[10,1,128]{2,1,0:T(1,128)S(1)}, f32[10,1,128]{2,1,0:T(1,128)S(1)}, u32[]{:S(2)}, u32[]{:S(2)}) collective-permute-start(f32[10,1,128]{2,1,0:T(1,128)S(1)} %get-tuple-element.48), channel_id=1, source_target_pairs={{0,1},{1,2},{2,3},{3,0},{4,5},{5,6},{6,7},{7,4},{8,9},{9,10},{10,1... | collective-permute-start | bytes 15368 | tf_op jit(solution)/shard_map/ppermute | solution.py:23
  262.5 5.4 %collective-permute-start.35 = (f32[10,1,128]{2,1,0:T(1,128)S(1)}, f32[10,1,128]{2,1,0:T(1,128)S(1)}, u32[]{:S(2)}, u32[]{:S(2)}) collective-permute-start(f32[10,1,128]{2,1,0:T(1,128)S(1)} %get-tuple-element.46), channel_id=1, source_target_pairs={{0,1},{1,2},{2,3},{3,0},{4,5},{5,6},{6,7},{7,4},{8,9},{9,10},{10,1... | collective-permute-start | bytes 15368 | tf_op jit(solution)/shard_map/ppermute | solution.py:23
  268.1 4.0 %collective-permute-start.37 = (f32[1,16,128]{2,1,0:T(8,128)S(1)}, f32[1,16,128]{2,1,0:T(8,128)S(1)}, u32[]{:S(2)}, u32[]{:S(2)}) collective-permute-start(f32[1,16,128]{2,1,0:T(8,128)S(1)} %get-tuple-element.53), channel_id=1, source_target_pairs={{0,4},{4,8},{8,12},{12,16},{16,20},{20,24},{24,28},{28,0},{1,5},{5... | collective-permute-start | bytes 24584 | tf_op jit(solution)/shard_map/ppermute | solution.py:23
  272.2 5.5 %collective-permute-start.39 = (f32[10,1,128]{2,1,0:T(1,128)S(1)}, f32[10,1,128]{2,1,0:T(1,128)S(1)}, u32[]{:S(2)}, u32[]{:S(2)}) collective-permute-start(f32[10,1,128]{2,1,0:T(1,128)S(1)} %get-tuple-element.44), channel_id=1, source_target_pairs={{0,1},{1,2},{2,3},{3,0},{4,5},{5,6},{6,7},{7,4},{8,9},{9,10},{10,1... | collective-permute-start | bytes 15368 | tf_op jit(solution)/shard_map/ppermute | solution.py:23
  (24 other events, 315.7 us)
where the time goes:
time: 279 us; the launch traced here: 278 us
  blocking collectives  167 us (60%)
  waiting for transfers between devices  50.3 us (18%)
  starting transfers between devices  48.6 us (17%)
  local copies, waits for them, and re-layouts  4.57 us (2%)
  other arithmetic  4.35 us (2%)
    psum x4, blocking collectives, global_sums(): return lax.psum(local, ('gx', 'gz'))  159 us
    ppermute x18, waiting for transfers between devices, with_halo(): before = lax.ppermute(last, axis, up)  34.2 us
    ppermute x18, starting transfers between devices, with_halo(): after = lax.ppermute(initial, axis, down)  27.8 us
    ppermute x18, starting transfers between devices, with_halo(): before = lax.ppermute(last, axis, up)  15.6 us
    ppermute x18, waiting for transfers between devices, with_halo(): after = lax.ppermute(initial, axis, down)  9.46 us
    unnamed x1, blocking collectives  8.52 us
    ppermute x4, waiting for transfers between devices, passed_along(): return lax.ppermute(value, axis, pairs)  6.56 us
  transfers between devices with their start and end apart: 40, of which 30 were waited for; matrix products, arithmetic and copies ran while one was open for 1% of the time, Pallas kernels for 0%

commit v1 on v0

--- a/solution.py
+++ b/solution.py
@@ -36,7 +36,7 @@
 
 def global_sums(pairs):
     local = jnp.stack([inner_local(left, right) for left, right in pairs])
-    return lax.psum(local, ("gx", "gz"))
+    return jnp.sum(lax.all_gather(local, ("gx", "gz")), axis=0)
 
 
 def solve_values(velocity_old, source, diag_coef, face_coef):

time: 279 us -> 363 us (1.30)
  blocking collectives: 167 us -> 252 us
    all_gather x0 -> x3, blocking collectives: none -> 204 us  [global_sums(): return jnp.sum(lax.all_gather(local, ('gx', 'gz')), axis=0)]
    psum x4 -> x0, blocking collectives: 159 us -> none  [global_sums(): return lax.psum(local, ('gx', 'gz'))]
    unnamed x1 -> x2, blocking collectives: 8.52 us -> 47.6 us
    ppermute x18, starting transfers between devices: 27.8 us -> 32 us  [with_halo(): after = lax.ppermute(initial, axis, down)]
    ppermute x18, starting transfers between devices: 15.6 us -> 11.7 us  [with_halo(): before = lax.ppermute(last, axis, up)]
  transfers between devices with their start and end apart: 40 -> 40, of which waited for: 30 -> 27; matrix products, arithmetic and copies ran while one was open for 1% -> 1% of each run, Pallas kernels for 0% -> 0%
where the time goes in v1:
time: 363 us
  blocking collectives  252 us (69%)
  waiting for transfers between devices  51.5 us (14%)
  starting transfers between devices  46.9 us (13%)
  local copies, waits for them, and re-layouts  4.86 us (1%)
  other arithmetic  4.52 us (1%)
    all_gather x3, blocking collectives, global_sums(): return jnp.sum(lax.all_gather(local, ('gx', 'gz')), axis=0)  204 us
    unnamed x2, blocking collectives  47.6 us
    ppermute x18, waiting for transfers between devices, with_halo(): before = lax.ppermute(last, axis, up)  34.8 us
    ppermute x18, starting transfers between devices, with_halo(): after = lax.ppermute(initial, axis, down)  32 us
    ppermute x18, starting transfers between devices, with_halo(): before = lax.ppermute(last, axis, up)  11.7 us
    ppermute x18, waiting for transfers between devices, with_halo(): after = lax.ppermute(initial, axis, down)  8.77 us
    ppermute x4, waiting for transfers between devices, passed_along(): return lax.ppermute(value, axis, pairs)  7.9 us
  transfers between devices with their start and end apart: 40, of which 27 were waited for; matrix products, arithmetic and copies ran while one was open for 1% of the time, Pallas kernels for 0%

profile of v1, /device:TPU:0, one launch (start us, length us, event | category | flops | bytes accessed | tf_op | source)
XLA Modules:
  0.0 362.9 jit_solution(10108983711025950101)
XLA Ops:
  1.6 3.1 collective-permute-start.3
  4.8 2.6 collective-permute-start.2
  9.5 2.6 collective-permute-done
  13.8 2.2 collective-permute-start.5
  18.1 2.6 collective-permute-start.7
  23.9 2.5 collective-permute-start.9
  28.4 68.1 %all-gather.4 = f32[32,2,3]{2,1,0:T(2,128)S(1)} all-gather(f32[1,2,3]{2,1,0:T(2,128)S(1)} %maximum_bitcast_fusion.1), channel_id=2, replica_groups=mesh['gx'=8,'gz'=4] {'gx','gz'}, dimensions={0}, use_global_device_ids=true | all-gather | bytes 792 | tf_op jit(solution)/shard_map/all_gather | solution.py:39
  96.7 2.6 collective-permute-start.11
  101.0 3.8 %collective-permute-start.13 = (f32[3,10,1,128]{3,2,1,0:T(1,128)S(1)}, f32[3,10,1,128]{3,2,1,0:T(1,128)S(1)}, u32[]{:S(2)}, u32[]{:S(2)}) collective-permute-start(f32[3,10,1,128]{3,2,1,0:T(1,128)S(1)} %get-tuple-element.23), channel_id=1, source_target_pairs={{1,0},{2,1},{3,2},{0,3},{5,4},{6,5},{7,6},{4,7},{9,8},{10,9},{11,1... | collective-permute-start | bytes 46088 | tf_op jit(solution)/shard_map/ppermute | solution.py:24
  106.8 68.2 %all-gather.5 = f32[32,4,3]{2,1,0:T(4,128)S(1)} all-gather(f32[1,4,3]{2,1,0:T(4,128)S(1)} %maximum_bitcast_fusion), channel_id=3, replica_groups=mesh['gx'=8,'gz'=4] {'gx','gz'}, dimensions={0}, use_global_device_ids=true | all-gather | bytes 1584 | tf_op jit(solution)/shard_map/all_gather | solution.py:39
  175.3 2.6 collective-permute-start.15
  179.6 3.8 %collective-permute-start.17 = (f32[3,10,1,128]{3,2,1,0:T(1,128)S(1)}, f32[3,10,1,128]{3,2,1,0:T(1,128)S(1)}, u32[]{:S(2)}, u32[]{:S(2)}) collective-permute-start(f32[3,10,1,128]{3,2,1,0:T(1,128)S(1)} %get-tuple-element.21), channel_id=1, source_target_pairs={{1,0},{2,1},{3,2},{0,3},{5,4},{6,5},{7,6},{4,7},{9,8},{10,9},{11,1... | collective-permute-start | bytes 46088 | tf_op jit(solution)/shard_map/ppermute | solution.py:24
  185.6 39.1 %all-reduce.19 = f32[96]{0:T(128)S(1)} all-reduce(f32[96]{0:T(128)S(1)} %dynamic-update-slice), channel_id=4, replica_groups=mesh['gx'=8,'gz'=4] {'gx','gz'}, use_global_device_ids=true, to_apply=%add.19 | all-reduce | flops 96 | bytes 768
  225.0 2.6 collective-permute-start.19
  229.2 2.2 collective-permute-start.20
  235.5 67.7 %all-gather.6 = f32[32,2,3]{2,1,0:T(2,128)S(1)} all-gather(f32[1,2,3]{2,1,0:T(2,128)S(1)} %maximum_bitcast_fusion.2), channel_id=5, replica_groups=mesh['gx'=8,'gz'=4] {'gx','gz'}, dimensions={0}, use_global_device_ids=true | all-gather | bytes 792 | tf_op jit(solution)/shard_map/all_gather | solution.py:39
  303.5 5.3 %collective-permute-done.23 = f32[8,1,128]{2,1,0:T(1,128)S(1)} collective-permute-done((f32[8,1,128]{2,1,0:T(1,128)S(1)}, f32[8,1,128]{2,1,0:T(1,128)S(1)}, u32[]{:S(2)}, u32[]{:S(2)}) %collective-permute-start.23) | collective-permute-done | bytes 4128 | tf_op jit(solution)/shard_map/ppermute | solution.py:13
  310.4 2.7 collective-permute-done.25
  313.1 2.4 collective-permute-start.26
  316.9 4.1 %collective-permute-done.27 = f32[10,1,128]{2,1,0:T(1,128)S(1)} collective-permute-done((f32[10,1,128]{2,1,0:T(1,128)S(1)}, f32[10,1,128]{2,1,0:T(1,128)S(1)}, u32[]{:S(2)}, u32[]{:S(2)}) %collective-permute-start.27) | collective-permute-done | bytes 5152 | tf_op jit(solution)/shard_map/ppermute | solution.py:23
  331.9 8.5 %all-reduce.20 = f32[64]{0:T(128)S(1)} all-reduce(f32[64]{0:T(128)S(1)} %convolution_bitcast_fusion), channel_id=6, replica_groups=mesh['gx'=8,'gz'=4] {'gz'}, use_global_device_ids=true, to_apply=%region_13.14.clone | all-reduce | flops 64 | bytes 512
  342.4 2.7 collective-permute-done.33
  348.7 3.7 %collective-permute-done.35 = f32[10,1,128]{2,1,0:T(1,128)S(1)} collective-permute-done((f32[10,1,128]{2,1,0:T(1,128)S(1)}, f32[10,1,128]{2,1,0:T(1,128)S(1)}, u32[]{:S(2)}, u32[]{:S(2)}) %collective-permute-start.35) | collective-permute-done | bytes 5152 | tf_op jit(solution)/shard_map/ppermute | solution.py:23
  353.9 2.7 collective-permute-done.37
  (170 shorter events, 52.4 us)
Async XLA Ops:
  1.6 7.8 %collective-permute-start.3 = (f32[8,1,128]{2,1,0:T(1,128)S(1)}, f32[8,1,128]{2,1,0:T(1,128)S(1)}, u32[]{:S(2)}, u32[]{:S(2)}) collective-permute-start(f32[8,1,128]{2,1,0:T(1,128)S(1)} %slice.567), channel_id=1, source_target_pairs={{0,1},{1,2},{2,3},{3,0},{4,5},{5,6},{6,7},{7,4},{8,9},{9,10},{10,1... | collective-permute-start | bytes 12296 | tf_op jit(solution)/shard_map/ppermute | solution.py:13
  4.7 7.3 %collective-permute-start.1 = (f32[3,1,16,128]{3,2,1,0:T(8,128)S(1)}, f32[3,1,16,128]{3,2,1,0:T(8,128)S(1)}, u32[]{:S(2)}, u32[]{:S(2)}) collective-permute-start(f32[3,1,16,128]{3,2,1,0:T(8,128)S(1)} %get-tuple-element.42), channel_id=1, source_target_pairs={{0,4},{4,8},{8,12},{12,16},{16,20},{20,24},{24,28},{28,0},{1,5},{5... | collective-permute-start | bytes 73736 | tf_op jit(solution)/shard_map/ppermute | solution.py:23
  4.8 7.4 %collective-permute-start.2 = (f32[3,1,16,128]{3,2,1,0:T(8,128)S(1)}, f32[3,1,16,128]{3,2,1,0:T(8,128)S(1)}, u32[]{:S(2)}, u32[]{:S(2)}) collective-permute-start(f32[3,1,16,128]{3,2,1,0:T(8,128)S(1)} %get-tuple-element.41), channel_id=1, source_target_pairs={{4,0},{8,4},{12,8},{16,12},{20,16},{24,20},{28,24},{0,28},{5,1},{9... | collective-permute-start | bytes 73736 | tf_op jit(solution)/shard_map/ppermute | solution.py:24
  12.2 5.6 %collective-permute-start.4 = (f32[3,10,1,128]{3,2,1,0:T(1,128)S(1)}, f32[3,10,1,128]{3,2,1,0:T(1,128)S(1)}, u32[]{:S(2)}, u32[]{:S(2)}) collective-permute-start(f32[3,10,1,128]{3,2,1,0:T(1,128)S(1)} %get-tuple-element.26), channel_id=1, source_target_pairs={{0,1},{1,2},{2,3},{3,0},{4,5},{5,6},{6,7},{7,4},{8,9},{9,10},{10,1... | collective-permute-start | bytes 46088 | tf_op jit(solution)/shard_map/ppermute | solution.py:23
  18.0 4.4 %collective-permute-start.6 = (f32[3,1,16,128]{3,2,1,0:T(8,128)S(1)}, f32[3,1,16,128]{3,2,1,0:T(8,128)S(1)}, u32[]{:S(2)}, u32[]{:S(2)}) collective-permute-start(f32[3,1,16,128]{3,2,1,0:T(8,128)S(1)} %get-tuple-element.36), channel_id=1, source_target_pairs={{0,4},{4,8},{8,12},{12,16},{16,20},{20,24},{24,28},{28,0},{1,5},{5... | collective-permute-start | bytes 73736 | tf_op jit(solution)/shard_map/ppermute | solution.py:23
  18.1 4.4 %collective-permute-start.7 = (f32[3,1,16,128]{3,2,1,0:T(8,128)S(1)}, f32[3,1,16,128]{3,2,1,0:T(8,128)S(1)}, u32[]{:S(2)}, u32[]{:S(2)}) collective-permute-start(f32[3,1,16,128]{3,2,1,0:T(8,128)S(1)} %get-tuple-element.37), channel_id=1, source_target_pairs={{4,0},{8,4},{12,8},{16,12},{20,16},{24,20},{28,24},{0,28},{5,1},{9... | collective-permute-start | bytes 73736 | tf_op jit(solution)/shard_map/ppermute | solution.py:24
  22.5 5.6 %collective-permute-start.8 = (f32[3,10,1,128]{3,2,1,0:T(1,128)S(1)}, f32[3,10,1,128]{3,2,1,0:T(1,128)S(1)}, u32[]{:S(2)}, u32[]{:S(2)}) collective-permute-start(f32[3,10,1,128]{3,2,1,0:T(1,128)S(1)} %get-tuple-element.24), channel_id=1, source_target_pairs={{0,1},{1,2},{2,3},{3,0},{4,5},{5,6},{6,7},{7,4},{8,9},{9,10},{10,1... | collective-permute-start | bytes 46088 | tf_op jit(solution)/shard_map/ppermute | solution.py:23
  23.9 4.2 %collective-permute-start.9 = (f32[3,10,1,128]{3,2,1,0:T(1,128)S(1)}, f32[3,10,1,128]{3,2,1,0:T(1,128)S(1)}, u32[]{:S(2)}, u32[]{:S(2)}) collective-permute-start(f32[3,10,1,128]{3,2,1,0:T(1,128)S(1)} %get-tuple-element.25), channel_id=1, source_target_pairs={{1,0},{2,1},{3,2},{0,3},{5,4},{6,5},{7,6},{4,7},{9,8},{10,9},{11,1... | collective-permute-start | bytes 46088 | tf_op jit(solution)/shard_map/ppermute | solution.py:24
  96.6 4.2 %collective-permute-start.10 = (f32[3,1,16,128]{3,2,1,0:T(8,128)S(1)}, f32[3,1,16,128]{3,2,1,0:T(8,128)S(1)}, u32[]{:S(2)}, u32[]{:S(2)}) collective-permute-start(f32[3,1,16,128]{3,2,1,0:T(8,128)S(1)} %get-tuple-element.34), channel_id=1, source_target_pairs={{0,4},{4,8},{8,12},{12,16},{16,20},{20,24},{24,28},{28,0},{1,5},{5... | collective-permute-start | bytes 73736 | tf_op jit(solution)/shard_map/ppermute | solution.py:23
  96.7 4.2 %collective-permute-start.11 = (f32[3,1,16,128]{3,2,1,0:T(8,128)S(1)}, f32[3,1,16,128]{3,2,1,0:T(8,128)S(1)}, u32[]{:S(2)}, u32[]{:S(2)}) collective-permute-start(f32[3,1,16,128]{3,2,1,0:T(8,128)S(1)} %get-tuple-element.35), channel_id=1, source_target_pairs={{4,0},{8,4},{12,8},{16,12},{20,16},{24,20},{28,24},{0,28},{5,1},{9... | collective-permute-start | bytes 73736 | tf_op jit(solution)/shard_map/ppermute | solution.py:24
  100.9 5.6 %collective-permute-start.12 = (f32[3,10,1,128]{3,2,1,0:T(1,128)S(1)}, f32[3,10,1,128]{3,2,1,0:T(1,128)S(1)}, u32[]{:S(2)}, u32[]{:S(2)}) collective-permute-start(f32[3,10,1,128]{3,2,1,0:T(1,128)S(1)} %get-tuple-element.22), channel_id=1, source_target_pairs={{0,1},{1,2},{2,3},{3,0},{4,5},{5,6},{6,7},{7,4},{8,9},{9,10},{10,1... | collective-permute-start | bytes 46088 | tf_op jit(solution)/shard_map/ppermute | solution.py:23
  101.0 5.5 %collective-permute-start.13 = (f32[3,10,1,128]{3,2,1,0:T(1,128)S(1)}, f32[3,10,1,128]{3,2,1,0:T(1,128)S(1)}, u32[]{:S(2)}, u32[]{:S(2)}) collective-permute-start(f32[3,10,1,128]{3,2,1,0:T(1,128)S(1)} %get-tuple-element.23), channel_id=1, source_target_pairs={{1,0},{2,1},{3,2},{0,3},{5,4},{6,5},{7,6},{4,7},{9,8},{10,9},{11,1... | collective-permute-start | bytes 46088 | tf_op jit(solution)/shard_map/ppermute | solution.py:24
  175.3 4.2 %collective-permute-start.14 = (f32[3,1,16,128]{3,2,1,0:T(8,128)S(1)}, f32[3,1,16,128]{3,2,1,0:T(8,128)S(1)}, u32[]{:S(2)}, u32[]{:S(2)}) collective-permute-start(f32[3,1,16,128]{3,2,1,0:T(8,128)S(1)} %get-tuple-element.32), channel_id=1, source_target_pairs={{0,4},{4,8},{8,12},{12,16},{16,20},{20,24},{24,28},{28,0},{1,5},{5... | collective-permute-start | bytes 73736 | tf_op jit(solution)/shard_map/ppermute | solution.py:23
  175.3 4.2 %collective-permute-start.15 = (f32[3,1,16,128]{3,2,1,0:T(8,128)S(1)}, f32[3,1,16,128]{3,2,1,0:T(8,128)S(1)}, u32[]{:S(2)}, u32[]{:S(2)}) collective-permute-start(f32[3,1,16,128]{3,2,1,0:T(8,128)S(1)} %get-tuple-element.33), channel_id=1, source_target_pairs={{4,0},{8,4},{12,8},{16,12},{20,16},{24,20},{28,24},{0,28},{5,1},{9... | collective-permute-start | bytes 73736 | tf_op jit(solution)/shard_map/ppermute | solution.py:24
  179.5 5.6 %collective-permute-start.16 = (f32[3,10,1,128]{3,2,1,0:T(1,128)S(1)}, f32[3,10,1,128]{3,2,1,0:T(1,128)S(1)}, u32[]{:S(2)}, u32[]{:S(2)}) collective-permute-start(f32[3,10,1,128]{3,2,1,0:T(1,128)S(1)} %get-tuple-element.20), channel_id=1, source_target_pairs={{0,1},{1,2},{2,3},{3,0},{4,5},{5,6},{6,7},{7,4},{8,9},{9,10},{10,1... | collective-permute-start | bytes 46088 | tf_op jit(solution)/shard_map/ppermute | solution.py:23
  179.6 5.5 %collective-permute-start.17 = (f32[3,10,1,128]{3,2,1,0:T(1,128)S(1)}, f32[3,10,1,128]{3,2,1,0:T(1,128)S(1)}, u32[]{:S(2)}, u32[]{:S(2)}) collective-permute-start(f32[3,10,1,128]{3,2,1,0:T(1,128)S(1)} %get-tuple-element.21), channel_id=1, source_target_pairs={{1,0},{2,1},{3,2},{0,3},{5,4},{6,5},{7,6},{4,7},{9,8},{10,9},{11,1... | collective-permute-start | bytes 46088 | tf_op jit(solution)/shard_map/ppermute | solution.py:24
  225.0 4.2 %collective-permute-start.18 = (f32[3,1,16,128]{3,2,1,0:T(8,128)S(1)}, f32[3,1,16,128]{3,2,1,0:T(8,128)S(1)}, u32[]{:S(2)}, u32[]{:S(2)}) collective-permute-start(f32[3,1,16,128]{3,2,1,0:T(8,128)S(1)} %get-tuple-element.30), channel_id=1, source_target_pairs={{0,4},{4,8},{8,12},{12,16},{16,20},{20,24},{24,28},{28,0},{1,5},{5... | collective-permute-start | bytes 73736 | tf_op jit(solution)/shard_map/ppermute | solution.py:23
  229.2 5.6 %collective-permute-start.20 = (f32[3,10,1,128]{3,2,1,0:T(1,128)S(1)}, f32[3,10,1,128]{3,2,1,0:T(1,128)S(1)}, u32[]{:S(2)}, u32[]{:S(2)}) collective-permute-start(f32[3,10,1,128]{3,2,1,0:T(1,128)S(1)} %get-tuple-element.18), channel_id=1, source_target_pairs={{0,1},{1,2},{2,3},{3,0},{4,5},{5,6},{6,7},{7,4},{8,9},{9,10},{10,1... | collective-permute-start | bytes 46088 | tf_op jit(solution)/shard_map/ppermute | solution.py:23
  303.4 5.5 %collective-permute-start.23 = (f32[8,1,128]{2,1,0:T(1,128)S(1)}, f32[8,1,128]{2,1,0:T(1,128)S(1)}, u32[]{:S(2)}, u32[]{:S(2)}) collective-permute-start(f32[8,1,128]{2,1,0:T(1,128)S(1)} %slice.610), channel_id=1, source_target_pairs={{0,1},{1,2},{2,3},{3,0},{4,5},{5,6},{6,7},{7,4},{8,9},{9,10},{10,1... | collective-permute-start | bytes 12296 | tf_op jit(solution)/shard_map/ppermute | solution.py:13
  303.4 5.4 %collective-permute-start.22 = (f32[1,16,128]{2,1,0:T(8,128)S(1)}, f32[1,16,128]{2,1,0:T(8,128)S(1)}, u32[]{:S(2)}, u32[]{:S(2)}) collective-permute-start(f32[1,16,128]{2,1,0:T(8,128)S(1)} %slice_bitcast_fusion.6), channel_id=1, source_target_pairs={{0,4},{4,8},{8,12},{12,16},{16,20},{20,24},{24,28},{28,0},{1,5},{5... | collective-permute-start | bytes 24584 | tf_op jit(solution)/shard_map/ppermute | solution.py:13
  315.5 5.4 %collective-permute-start.27 = (f32[10,1,128]{2,1,0:T(1,128)S(1)}, f32[10,1,128]{2,1,0:T(1,128)S(1)}, u32[]{:S(2)}, u32[]{:S(2)}) collective-permute-start(f32[10,1,128]{2,1,0:T(1,128)S(1)} %get-tuple-element.50), channel_id=1, source_target_pairs={{0,1},{1,2},{2,3},{3,0},{4,5},{5,6},{6,7},{7,4},{8,9},{9,10},{10,1... | collective-permute-start | bytes 15368 | tf_op jit(solution)/shard_map/ppermute | solution.py:23
  325.2 5.5 %collective-permute-start.31 = (f32[10,1,128]{2,1,0:T(1,128)S(1)}, f32[10,1,128]{2,1,0:T(1,128)S(1)}, u32[]{:S(2)}, u32[]{:S(2)}) collective-permute-start(f32[10,1,128]{2,1,0:T(1,128)S(1)} %get-tuple-element.48), channel_id=1, source_target_pairs={{0,1},{1,2},{2,3},{3,0},{4,5},{5,6},{6,7},{7,4},{8,9},{9,10},{10,1... | collective-permute-start | bytes 15368 | tf_op jit(solution)/shard_map/ppermute | solution.py:23
  347.0 5.4 %collective-permute-start.35 = (f32[10,1,128]{2,1,0:T(1,128)S(1)}, f32[10,1,128]{2,1,0:T(1,128)S(1)}, u32[]{:S(2)}, u32[]{:S(2)}) collective-permute-start(f32[10,1,128]{2,1,0:T(1,128)S(1)} %get-tuple-element.46), channel_id=1, source_target_pairs={{0,1},{1,2},{2,3},{3,0},{4,5},{5,6},{6,7},{7,4},{8,9},{9,10},{10,1... | collective-permute-start | bytes 15368 | tf_op jit(solution)/shard_map/ppermute | solution.py:23
  356.7 5.5 %collective-permute-start.39 = (f32[10,1,128]{2,1,0:T(1,128)S(1)}, f32[10,1,128]{2,1,0:T(1,128)S(1)}, u32[]{:S(2)}, u32[]{:S(2)}) collective-permute-start(f32[10,1,128]{2,1,0:T(1,128)S(1)} %get-tuple-element.44), channel_id=1, source_target_pairs={{0,1},{1,2},{2,3},{3,0},{4,5},{5,6},{6,7},{7,4},{8,9},{9,10},{10,1... | collective-permute-start | bytes 15368 | tf_op jit(solution)/shard_map/ppermute | solution.py:23
  (24 other events, 400.1 us)
